TPU v7x, 768 devices: a whole 4x8x12 slice. The times are simulated.
768 devices in a mesh: energy: 8 (over y), cell: 96 (over x, z, core).
Axes of the slice: x: 4, y: 8, z: 12, core: 2. Of those that a mesh axis runs over, the one named last changes fastest.
Arguments:
- green_less: float32 [2, 8, 96, 320, 320], P(None, None, 'cell', 'energy'), may hold values from -6 to 6
- green_greater: float32 [2, 8, 96, 320, 320], P(None, None, 'cell', 'energy'), may hold values from -6 to 6
- offsets: int32 [8], replicated, may hold values from 0 to 7, as said below
- orbitals: int32 [96], replicated, may hold values from 192 to 320
- coulomb_diag: float32 [96, 320, 320], P('cell'), may hold values from -0.3125 to 0.3125
- coulomb_up: float32 [96, 320, 320], P('cell'), may hold values from -0.3125 to 0.3125
Outputs:
- screened_diag: float32 [2, 8, 96, 320, 320], P(None, 'energy', 'cell')
- screened_up: float32 [2, 8, 96, 320, 320], P(None, 'energy', 'cell')
Inputs may be any that keep to these rules, and one draw needn't show every extreme that they name: offsets is a permutation of 0 to 7.
All inputs are finite; a program needn't handle non-finite values.
Results may differ from a plain program's by a relative error of at most 0.0003.
Values sent between devices are 32-bit elements; how exact they have to be, the bound alone decides.
No kernel may reach another device: no remote copies, remote signals or barrier semaphores. Data moves between devices by JAX's collectives and lax.ppermute only.
A program may use at most 32 MiB of HBM per device.

v0:
```python
import math

import jax
import jax.numpy as jnp
from jax import lax
from jax.sharding import PartitionSpec as P

HIGH = lax.Precision.HIGHEST


def from_behind(block, axis, distance):
    devices = range(lax.axis_size(axis))
    route = [(i - distance, i) for i in devices if i - distance in devices]
    return lax.ppermute(block, axis, route)


def polarize(lesser, greater, offsets):
    count = lesser.shape[1]
    energies = jnp.arange(count, dtype=jnp.int32)

    def single(shift):
        source = energies - shift
        weight = (source >= 0).astype(jnp.float32)
        picked = jnp.take(greater, jnp.clip(source, 0, count - 1), axis=1)
        real_part = lesser[0] * picked[0] + lesser[1] * picked[1]
        imag_part = lesser[1] * picked[0] - lesser[0] * picked[1]
        weight = weight.reshape((count,) + (1,) * (lesser.ndim - 2))
        return jnp.stack([jnp.sum(real_part * weight, axis=0), jnp.sum(imag_part * weight, axis=0)])

    return lax.map(single, offsets) / math.sqrt(count)


def left_mul(coupling, blocks):
    return jnp.einsum("ij,ejk->eik", coupling, blocks, precision=HIGH)


def left_mul_t(coupling, blocks):
    return jnp.einsum("ji,ejk->eik", coupling, blocks, precision=HIGH)


def right_mul(blocks, coupling):
    return jnp.einsum("eij,jk->eik", blocks, coupling, precision=HIGH)


def right_mul_t(blocks, coupling):
    return jnp.einsum("eij,kj->eik", blocks, coupling, precision=HIGH)


def per_device(green_less, green_greater, offsets, orbitals, coulomb_diag, coulomb_up):
    polar = polarize(green_less, green_greater, offsets)
    owned = lax.all_to_all(polar, "energy", split_axis=0, concat_axis=3, tiled=True)
    width = owned.shape[-1]
    en_count = owned.shape[0]
    local = owned.reshape(en_count * 2, width, width)
    cell_index = lax.axis_index("cell")
    cell_count = lax.axis_size("cell")
    rows = jnp.arange(width, dtype=jnp.int32)
    orbit_here = jnp.take(orbitals, cell_index)
    orbit_next = jnp.take(orbitals, jnp.minimum(cell_index + 1, cell_count - 1))
    inside = (rows < orbit_here).astype(jnp.float32)
    inside_next = (rows < orbit_next).astype(jnp.float32)
    vdiag = coulomb_diag[0] * inside[:, None] * inside[None, :]
    vup = coulomb_up[0] * inside[:, None] * inside_next[None, :]
    below = from_behind(jnp.concatenate([local, vup[None]], 0), "cell", 1)
    above = from_behind(jnp.concatenate([local, vdiag[None]], 0), "cell", -1)
    prev_polar = below[:-1]
    prev_up = below[-1]
    next_polar = above[:-1]
    next_diag = above[-1]
    keep = (cell_index < cell_count - 1).astype(jnp.float32)
    a_here = left_mul(vdiag, local)
    a_next = left_mul(vup, next_polar)
    diag = (
        right_mul_t(a_here, vdiag)
        + right_mul_t(a_next, vup)
        + right_mul(left_mul_t(prev_up, prev_polar), prev_up)
    )
    upper = right_mul(a_here, vup) * keep + right_mul_t(a_next, next_diag)
    diag = jnp.moveaxis(diag.reshape(en_count, 2, width, width), 0, 1)[:, :, None]
    upper = jnp.moveaxis(upper.reshape(en_count, 2, width, width), 0, 1)[:, :, None]
    return (diag, upper)


def solution(mesh):
    in_specs = (
        P(None, None, "cell", "energy", None),
        P(None, None, "cell", "energy", None),
        P(),
        P(),
        P("cell", None, None),
        P("cell", None, None),
    )
    out_specs = (P(None, "energy", "cell", None, None), P(None, "energy", "cell", None, None))
    return jax.shard_map(
        per_device, mesh=mesh, in_specs=in_specs, out_specs=out_specs, check_vma=False
    )
```

profile of v0, /device:TPU:6, one launch (start us, length us, event | category | flops | bytes accessed | tf_op | source)
XLA Modules:
  0.0 125.6 jit_solution(700265059242305549)
XLA Ops:
  0.6 41.5 %while.13 = (s32[]{:T(128)}, f32[8,2,1,40,320]{4,3,2,1,0:T(8,128)S(1)}, f32[2,8,1,40,320]{4,3,2,1,0:T(8,128)}, s32[8]{0:T(128)}, f32[2,8,1,40,320]{4,3,2,1,0:T(8,128)}, /*index=5*/s32[]{:T(128)}) while((s32[]{:T(128)}, f32[8,2,1,40,320]{4,3,2,1,0:T(8,128)S(1)}, f32[2,8,1,40,320]{4,3,2,1,0:T(8,128)}, s32[8]{0:T(128)}, ...), condition=%wide.region_3.4_spmd.clone, body=%wide.region_0.3_spmd.clone.sunk | while | flops 1229946 | bytes 8544553 | solution.py:30
  0.7 1.2 dynamic_slice.6
  2.6 1.8 %gather_fusion = f32[8,2,40,320]{3,2,1,0:T(8,128)S(1)} fusion(f32[2,8,40,320]{3,2,1,0:T(8,128)} %bitcast.149, s32[1024]{0:T(1024)S(1)} %pad_clamp_fusion.2), kind=kCustom, calls=%fused_computation.clone.clone.1 | custom fusion | bytes 1638432 | tf_op jit(solution)/shard_map/while/body/eval_jaxpr/jit(_take)/gather | solution.py:24
  5.8 1.2 dynamic_slice.6
  7.7 1.8 %gather_fusion = f32[8,2,40,320]{3,2,1,0:T(8,128)S(1)} fusion(f32[2,8,40,320]{3,2,1,0:T(8,128)} %bitcast.149, s32[1024]{0:T(1024)S(1)} %pad_clamp_fusion.2), kind=kCustom, calls=%fused_computation.clone.clone.1 | custom fusion | bytes 1638432 | tf_op jit(solution)/shard_map/while/body/eval_jaxpr/jit(_take)/gather | solution.py:24
  11.0 1.2 dynamic_slice.6
  12.9 1.8 %gather_fusion = f32[8,2,40,320]{3,2,1,0:T(8,128)S(1)} fusion(f32[2,8,40,320]{3,2,1,0:T(8,128)} %bitcast.149, s32[1024]{0:T(1024)S(1)} %pad_clamp_fusion.2), kind=kCustom, calls=%fused_computation.clone.clone.1 | custom fusion | bytes 1638432 | tf_op jit(solution)/shard_map/while/body/eval_jaxpr/jit(_take)/gather | solution.py:24
  16.2 1.2 dynamic_slice.6
  18.1 1.8 %gather_fusion = f32[8,2,40,320]{3,2,1,0:T(8,128)S(1)} fusion(f32[2,8,40,320]{3,2,1,0:T(8,128)} %bitcast.149, s32[1024]{0:T(1024)S(1)} %pad_clamp_fusion.2), kind=kCustom, calls=%fused_computation.clone.clone.1 | custom fusion | bytes 1638432 | tf_op jit(solution)/shard_map/while/body/eval_jaxpr/jit(_take)/gather | solution.py:24
  21.4 1.2 dynamic_slice.6
  23.3 1.8 %gather_fusion = f32[8,2,40,320]{3,2,1,0:T(8,128)S(1)} fusion(f32[2,8,40,320]{3,2,1,0:T(8,128)} %bitcast.149, s32[1024]{0:T(1024)S(1)} %pad_clamp_fusion.2), kind=kCustom, calls=%fused_computation.clone.clone.1 | custom fusion | bytes 1638432 | tf_op jit(solution)/shard_map/while/body/eval_jaxpr/jit(_take)/gather | solution.py:24
  26.6 1.2 dynamic_slice.6
  28.5 1.8 %gather_fusion = f32[8,2,40,320]{3,2,1,0:T(8,128)S(1)} fusion(f32[2,8,40,320]{3,2,1,0:T(8,128)} %bitcast.149, s32[1024]{0:T(1024)S(1)} %pad_clamp_fusion.2), kind=kCustom, calls=%fused_computation.clone.clone.1 | custom fusion | bytes 1638432 | tf_op jit(solution)/shard_map/while/body/eval_jaxpr/jit(_take)/gather | solution.py:24
  31.8 1.2 dynamic_slice.6
  33.7 1.8 %gather_fusion = f32[8,2,40,320]{3,2,1,0:T(8,128)S(1)} fusion(f32[2,8,40,320]{3,2,1,0:T(8,128)} %bitcast.149, s32[1024]{0:T(1024)S(1)} %pad_clamp_fusion.2), kind=kCustom, calls=%fused_computation.clone.clone.1 | custom fusion | bytes 1638432 | tf_op jit(solution)/shard_map/while/body/eval_jaxpr/jit(_take)/gather | solution.py:24
  36.9 1.2 dynamic_slice.6
  38.9 1.8 %gather_fusion = f32[8,2,40,320]{3,2,1,0:T(8,128)S(1)} fusion(f32[2,8,40,320]{3,2,1,0:T(8,128)} %bitcast.149, s32[1024]{0:T(1024)S(1)} %pad_clamp_fusion.2), kind=kCustom, calls=%fused_computation.clone.clone.1 | custom fusion | bytes 1638432 | tf_op jit(solution)/shard_map/while/body/eval_jaxpr/jit(_take)/gather | solution.py:24
  43.2 7.2 %all-to-all-start = ((f32[8,2,1,40,320]{4,3,1,2,0:T(8,128)}), f32[8,2,1,40,320]{4,3,1,2,0:T(8,128)S(1)}, u32[]{:S(2)}, u32[]{:S(2)}) async-start(f32[8,2,1,40,320]{4,3,1,2,0:T(8,128)} %bitcast_multiply_fusion.4), calls=%async_computation | async-start | bytes 1966080 | tf_op jit(solution)/shard_map/all_to_all | solution.py:51
  53.9 23.8 %all-to-all-done = f32[8,2,1,40,320]{4,3,1,2,0:T(8,128)S(1)} async-done(((f32[8,2,1,40,320]{4,3,1,2,0:T(8,128)}), f32[8,2,1,40,320]{4,3,1,2,0:T(8,128)S(1)}, u32[]{:S(2)}, u32[]{:S(2)}) %all-to-all-start) | async-done | bytes 819232 | tf_op jit(solution)/shard_map/all_to_all | solution.py:51
  78.1 1.2 pad_maximum_fusion
  79.4 14.5 %collective-permute-start = (f32[3,320,320]{1,2,0:T(8,128)}, f32[3,320,320]{1,2,0:T(8,128)S(1)}, u32[]{:S(2)}, u32[]{:S(2)}) collective-permute-start(f32[3,320,320]{1,2,0:T(8,128)} %pad_maximum_fusion), channel_id=1, source_target_pairs={{1,0},{2,1},{3,2},{4,3},{5,4},{6,5},{7,6},{8,7},{9,8},{10,9},{11,1... | collective-permute-start | bytes 3686408 | tf_op jit(solution)/shard_map/ppermute | solution.py:14
  93.8 2.0 %copy.61 = f32[1,320,320]{2,1,0:T(8,128)} copy(f32[1,320,320]{1,2,0:T(8,128)} %get-tuple-element.89) | data formatting | bytes 819200 | tf_op jit(solution)/shard_map/mul | solution.py:63
  97.0 2.2 %collective-permute-start.1 = (f32[3,320,320]{2,1,0:T(8,128)S(1)}, f32[3,320,320]{2,1,0:T(8,128)S(1)}, u32[]{:S(2)}, u32[]{:S(2)}) collective-permute-start(f32[3,320,320]{2,1,0:T(8,128)S(1)} %pad_maximum_fusion.1), channel_id=1, source_target_pairs={{0,1},{1,2},{2,3},{3,4},{4,5},{5,6},{6,7},{7,8},{8,9},{9,10},{10,1... | collective-permute-start | bytes 3686408 | tf_op jit(solution)/shard_map/ppermute | solution.py:14
  99.3 2.2 %convolution_bitcast_fusion.2 = f32[2,320,320]{1,2,0:T(8,128)S(1)} fusion(f32[2,320,320]{2,1,0:T(8,128)S(1)} %bitcast.152, f32[1,320,320]{1,2,0:T(8,128)S(1)} %get-tuple-element.90), kind=kOutput, calls=%fused_computation.32 | convolution fusion | flops 786432000 | bytes 2048000 | tf_op jit(solution)/shard_map/ij,ejk->eik/dot_general | solution.py:34
  101.5 3.7 %fusion.16 = f32[2,320,320]{2,1,0:T(8,128)S(1)} fusion(f32[2,320,320]{1,2,0:T(8,128)S(1)} %convolution_bitcast_fusion.2, f32[1,320,320]{2,1,0:T(8,128)S(1)} %copy-done.3, f32[320]{0:T(512)S(1)} %get-tuple-element.93), kind=kOutput, calls=%fused_computation.42 | convolution fusion | flops 786636800 | bytes 2049280 | tf_op jit(solution)/shard_map/eij,kj->eik/dot_general | solution.py:46
  105.2 2.3 %convolution_multiply_fusion = f32[2,320,320]{2,1,0:T(8,128)S(1)} fusion(f32[2,320,320]{1,2,0:T(8,128)S(1)} %convolution_bitcast_fusion.2, f32[]{:T(128)S(6)} %convert_element_type.30, f32[1,320,320]{2,1,0:T(8,128)S(1)} %copy-done.1, f32[320]{0:T(512)S(1)} %get-tuple-element.94, f32[320]{0:T(512)S(1)} %get-tuple-element.93), kind=kOutput, calls=%fused_computation.26 | convolution fusion | flops 786841600 | bytes 2050564 | tf_op jit(solution)/shard_map/eij,jk->eik/dot_general | solution.py:42
  107.5 3.5 %collective-permute-done = f32[3,320,320]{1,2,0:T(8,128)S(1)} collective-permute-done((f32[3,320,320]{1,2,0:T(8,128)}, f32[3,320,320]{1,2,0:T(8,128)S(1)}, u32[]{:S(2)}, u32[]{:S(2)}) %collective-permute-start) | collective-permute-done | bytes 1228832 | tf_op jit(solution)/shard_map/ppermute | solution.py:14
  111.0 2.1 %convolution_bitcast_fusion.1 = f32[2,320,320]{1,2,0:T(8,128)S(1)} fusion(f32[3,320,320]{1,2,0:T(8,128)S(1)} %collective-permute-done, f32[1,320,320]{2,1,0:T(8,128)S(1)} %copy-done.1, f32[320]{0:T(512)S(1)} %get-tuple-element.94, f32[320]{0:T(512)S(1)} %get-tuple-element.93), kind=kOutput, calls=%fused_computation.31 | convolution fusion | flops 786636800 | bytes 2460160 | tf_op jit(solution)/shard_map/ij,ejk->eik/dot_general | solution.py:34
  113.1 3.4 %fusion.9 = f32[2,1,1,320,320]{4,3,2,1,0:T(8,128)} fusion(f32[2,320,320]{2,1,0:T(8,128)S(1)} %convolution_multiply_fusion, f32[2,320,320]{1,2,0:T(8,128)S(1)} %convolution_bitcast_fusion.1, f32[3,320,320]{1,2,0:T(8,128)S(1)} %collective-permute-done), kind=kOutput, calls=%fused_computation.25 | convolution fusion | flops 786636800 | bytes 3276800 | tf_op jit(solution)/shard_map/eij,kj->eik/dot_general | solution.py:46
  116.5 3.7 %convolution_add_fusion.2 = f32[2,320,320]{2,1,0:T(8,128)S(1)} fusion(f32[2,320,320]{2,1,0:T(8,128)S(1)} %fusion.16, f32[2,320,320]{1,2,0:T(8,128)S(1)} %convolution_bitcast_fusion.1, f32[1,320,320]{2,1,0:T(8,128)S(1)} %copy-done.1, f32[320]{0:T(512)S(1)} %get-tuple-element.94, f32[320]{0:T(512)S(1)} %get-tuple-element.93), kind=kOutput, calls=%fused_computation.29 | convolution fusion | flops 786841600 | bytes 2869760 | tf_op jit(solution)/shard_map/eij,kj->eik/dot_general | solution.py:46
  120.2 2.2 %convolution_bitcast_fusion = f32[2,320,320]{1,2,0:T(8,128)S(1)} fusion(f32[3,320,320]{2,1,0:T(8,128)S(1)} %collective-permute-done.1), kind=kOutput, calls=%fused_computation.30 | convolution fusion | flops 786432000 | bytes 2785280 | tf_op jit(solution)/shard_map/ji,ejk->eik/dot_general | solution.py:38
  122.4 3.2 %fusion.10 = f32[2,1,1,320,320]{4,3,2,1,0:T(8,128)} fusion(f32[2,320,320]{2,1,0:T(8,128)S(1)} %convolution_add_fusion.2, f32[2,320,320]{1,2,0:T(8,128)S(1)} %convolution_bitcast_fusion, f32[3,320,320]{2,1,0:T(8,128)S(1)} %collective-permute-done.1), kind=kOutput, calls=%fused_computation.28 | convolution fusion | flops 786636800 | bytes 3276800 | tf_op jit(solution)/shard_map/eij,jk->eik/dot_general | solution.py:42
  (83 shorter events, 21.3 us)
Async XLA Ops:
  4.4 1.2 copy-start
  9.6 1.2 copy-start
  14.8 1.2 copy-start
  19.9 1.2 copy-start
  25.1 1.2 copy-start
  30.3 1.2 copy-start
  35.5 1.2 copy-start
  40.7 1.2 copy-start
  43.1 7.3 %copy-start.2 = (f32[1,320,320]{2,1,0:T(8,128)S(1)}, f32[1,320,320]{2,1,0:T(8,128)}, u32[]{:S(2)}) copy-start(f32[1,320,320]{2,1,0:T(8,128)} %param.12) | copy-start | bytes 1228804
  43.2 7.5 %copy-start.1 = (f32[1,320,320]{2,1,0:T(8,128)S(1)}, f32[1,320,320]{2,1,0:T(8,128)}, u32[]{:S(2)}) copy-start(f32[1,320,320]{2,1,0:T(8,128)} %param.13) | copy-start | bytes 1228804
  43.2 34.6 %all-to-all-start = ((f32[8,2,1,40,320]{4,3,1,2,0:T(8,128)}), f32[8,2,1,40,320]{4,3,1,2,0:T(8,128)S(1)}, u32[]{:S(2)}, u32[]{:S(2)}) async-start(f32[8,2,1,40,320]{4,3,1,2,0:T(8,128)} %bitcast_multiply_fusion.4), calls=%async_computation | async-start | bytes 1966080 | tf_op jit(solution)/shard_map/all_to_all | solution.py:51
  50.4 0.7 copy-start.4
  79.4 31.6 %collective-permute-start = (f32[3,320,320]{1,2,0:T(8,128)}, f32[3,320,320]{1,2,0:T(8,128)S(1)}, u32[]{:S(2)}, u32[]{:S(2)}) collective-permute-start(f32[3,320,320]{1,2,0:T(8,128)} %pad_maximum_fusion), channel_id=1, source_target_pairs={{1,0},{2,1},{3,2},{4,3},{5,4},{6,5},{7,6},{8,7},{9,8},{10,9},{11,1... | collective-permute-start | bytes 3686408 | tf_op jit(solution)/shard_map/ppermute | solution.py:14
  97.0 4.5 %copy-start.3 = (f32[1,320,320]{2,1,0:T(8,128)S(1)}, f32[1,320,320]{2,1,0:T(8,128)}, u32[]{:S(2)}) copy-start(f32[1,320,320]{2,1,0:T(8,128)} %param.12) | copy-start | bytes 1228804
  97.0 23.2 %collective-permute-start.1 = (f32[3,320,320]{2,1,0:T(8,128)S(1)}, f32[3,320,320]{2,1,0:T(8,128)S(1)}, u32[]{:S(2)}, u32[]{:S(2)}) collective-permute-start(f32[3,320,320]{2,1,0:T(8,128)S(1)} %pad_maximum_fusion.1), channel_id=1, source_target_pairs={{0,1},{1,2},{2,3},{3,4},{4,5},{5,6},{6,7},{7,8},{8,9},{9,10},{10,1... | collective-permute-start | bytes 3686408 | tf_op jit(solution)/shard_map/ppermute | solution.py:14
where the time goes:
time: 127 us; the launch traced here: 126 us
  local copies, waits for them, and re-layouts  30.8 us (24%)
  waiting for transfers between devices  27.4 us (22%)
  starting transfers between devices  23.9 us (19%)
  matrix products  22.7 us (18%)
  other arithmetic  18.2 us (14%)
  between operations  2.06 us (2%)
    all_to_all x1, waiting for transfers between devices, per_device(): lax.all_to_all(polar, 'energy', split_axis=0, concat_axis=3, tiled=True)  23.8 us
    ppermute x2, starting transfers between devices, from_behind(): return lax.ppermute(block, axis, route)  16.7 us
    gather x8, local copies, waits for them, and re-layouts, single(): picked = jnp.take(greater, jnp.clip(source, 0, count - 1), axis=1)  14.5 us
    dot_general x3, matrix products, right_mul_t(): return jnp.einsum('eij,kj->eik', blocks, coupling, precision=HIGH)  10.8 us
    dynamic_slice x8, local copies, waits for them, and re-layouts, polarize(): return lax.map(single, offsets) / math.sqrt(count)  9.94 us
    all_to_all x1, starting transfers between devices, per_device(): lax.all_to_all(polar, 'energy', split_axis=0, concat_axis=3, tiled=True)  7.23 us
    select_n x16, other arithmetic, single(): picked = jnp.take(greater, jnp.clip(source, 0, count - 1), axis=1)  6.28 us
    convert_element_type x8, other arithmetic, single(): weight = (source >= 0).astype(jnp.float32)  5.92 us
  transfers between devices with their start and end apart: 3, of which 2 were waited for; matrix products, arithmetic and copies ran while one was open for 18% of the time, Pallas kernels for 0%

commit v1 on v0

v1 whole, which is shorter than its diff:
```python
import functools
import math

import jax
import jax.numpy as jnp
from jax import lax
from jax.experimental import pallas as pl
from jax.experimental.pallas import tpu as pltpu
from jax.sharding import PartitionSpec as P

F32, BF16 = jnp.float32, jnp.bfloat16
LANES = 128
VMEM = pl.BlockSpec(memory_space=pltpu.VMEM)
SMEM = pl.BlockSpec(memory_space=pltpu.SMEM)


def params(mib):
    return pltpu.CompilerParams(vmem_limit_bytes=mib << 20)


def cost(flops, moved):
    return pl.CostEstimate(flops=flops, bytes_accessed=moved, transcendentals=0)


def shift_cells(block, distance):
    devices = range(lax.axis_size("cell"))
    route = [(i - distance, i) for i in devices if i - distance in devices]
    return lax.ppermute(block, "cell", route)


def lag_products(less, greater, count):
    scale = 1.0 / math.sqrt(count)
    for lag in range(count):
        real = imag = None
        for m in range(lag, count):
            lr, li = less(0, m), less(1, m)
            gr, gi = greater(0, m - lag), greater(1, m - lag)
            re = lr * gr + li * gi
            im = li * gr - lr * gi
            real = re if real is None else real + re
            imag = im if imag is None else imag + im
        yield lag, real * scale, imag * scale


def polar_kernel(first, count, rows, offsets, less, greater, out, slot):
    for n in range(count):
        slot[offsets[n]] = n
    tail = less.shape[-1] % LANES

    def group(g, carry):
        at = pl.ds(pl.multiple_of(g * 8, 8), 8)
        if first:
            columns = pl.ds(LANES, LANES)
        else:
            columns = pl.ds(0, LANES)
        read = lambda ref: (lambda part, m: ref[part, m, 0, at, columns])
        for lag, real, imag in lag_products(read(less), read(greater), count):
            n = slot[lag]
            out[n, 0, at, :] = real
            out[n, 1, at, :] = imag
        if first:
            last = pl.ds(2 * LANES, tail)
            read = lambda ref: (lambda part, m: ref[part, m, 0, at, last])
            for lag, real, imag in lag_products(read(less), read(greater), count):
                out[slot[lag], 2, at, :] = jnp.concatenate([real, imag], axis=-1)
        return carry

    lax.fori_loop(0, rows // 8, group, 0)


def polarize(first, offsets, less, greater):
    _, count, _, rows, width = less.shape
    tiles = 3 if first else 2
    return pl.pallas_call(
        functools.partial(polar_kernel, first, count, rows),
        out_shape=jax.ShapeDtypeStruct((count, tiles, rows, LANES), F32),
        in_specs=[SMEM, VMEM, VMEM],
        out_specs=VMEM,
        scratch_shapes=[pltpu.SMEM((count,), jnp.int32)],
        compiler_params=params(24),
        cost_estimate=cost(36 * 8 * rows * tiles * LANES, 3_000_000),
        name="polar_a" if first else "polar_b",
    )(offsets, less, greater)


def halves(x):
    high = x.astype(BF16)
    return high, (x - high.astype(F32)).astype(BF16)


def dot3(a, b, dims):
    (ah, al), (bh, bl) = a, b
    dot = lambda x, y: lax.dot_general(x, y, (dims, ((), ())), preferred_element_type=F32)
    return dot(ah, bh) + (dot(ah, bl) + dot(al, bh))


NN, NT, TN = ((1,), (0,)), ((1,), (1,)), ((0,), (0,))


def prep_kernel(sizes, diag, up, prev_up, next_diag, diag_o, up_o, prev_o, prevt_o, next_o):
    size = diag.shape[1]
    row = lax.broadcasted_iota(jnp.int32, (size, size), 0)
    col = lax.broadcasted_iota(jnp.int32, (size, size), 1)

    def put(out, x):
        high, low = halves(x)
        out[0], out[1] = high, low

    prev, here, after, after_up = sizes[0], sizes[1], sizes[2], sizes[3]
    put(diag_o, jnp.where((row < here) & (col < here), diag[0], 0.0))
    put(up_o, jnp.where((row < here) & (col < after_up), up[0], 0.0))
    masked = jnp.where((row < prev) & (col < here), prev_up[0], 0.0)
    put(prev_o, masked)
    put(prevt_o, masked.T)
    put(next_o, jnp.where((row < after) & (col < after), next_diag[0], 0.0))


def prepare(sizes, diag, up, prev_up, next_diag):
    size = diag.shape[1]
    out = jax.ShapeDtypeStruct((2, size, size), BF16)
    return pl.pallas_call(
        prep_kernel,
        out_shape=(out,) * 5,
        in_specs=[SMEM] + [VMEM] * 4,
        out_specs=(VMEM,) * 5,
        compiler_params=params(24),
        cost_estimate=cost(8 * 5 * size * size, 5 * 8 * size * size),
        name="prep",
    )(sizes, diag, up, prev_up, next_diag)


def columns_of(tiles):
    return (LANES, 3 * LANES - LANES // 2) if tiles == 3 else (0, LANES)


def block_of(ref):
    src, tiles, rows, lanes = ref.shape
    return jnp.concatenate([ref[:, t].reshape(src * rows, lanes) for t in range(tiles)], axis=1)


def times_block(left, ref):
    product = dot3((left[0], left[1]), halves(block_of(ref)), NN)
    real, imag = product[:, :LANES], product[:, LANES : 2 * LANES]
    if product.shape[1] > 2 * LANES:
        rest, half = product[:, 2 * LANES :], LANES // 2
        real = jnp.concatenate([real, rest[:, :half]], axis=1)
        imag = jnp.concatenate([imag, rest[:, half:]], axis=1)
    return halves(jnp.concatenate([real, imag], axis=0))


def rows_of(ref, lo, hi):
    return ref[0, lo:hi, :], ref[1, lo:hi, :]


def cols_of(ref, lo, hi):
    return ref[0, :, lo:hi], ref[1, :, lo:hi]


def put_sum(out, before, value):
    size = out.shape[-1]
    value = value.reshape(2, size, size)
    for part in range(2):
        out[part] = value[part] if before is None else before[part] + value[part]


def here_kernel(chunk_a, chunk_b, diag, up, diag_out, up_out):
    total_d = total_u = None
    for chunk in (chunk_a, chunk_b):
        lo, hi = columns_of(chunk.shape[1])
        left = times_block(diag, chunk)
        d = dot3(left, cols_of(diag, lo, hi), NT)
        u = dot3(left, rows_of(up, lo, hi), NN)
        total_d = d if total_d is None else total_d + d
        total_u = u if total_u is None else total_u + u
    put_sum(diag_out, None, total_d)
    put_sum(up_out, None, total_u)


def around_kernel(prev_p, next_p, up, prev_up, prev_upt, next_diag, diag_in, up_in, diag_out, up_out):
    lo, hi = columns_of(prev_p.shape[1])
    left = times_block(up, next_p)
    put_sum(up_out, up_in, dot3(left, cols_of(next_diag, lo, hi), NT))
    total = dot3(left, cols_of(up, lo, hi), NT)
    left = times_block(prev_upt, prev_p)
    put_sum(diag_out, diag_in, total + dot3(left, rows_of(prev_up, lo, hi), NN))


def products(kernel, name, operands, size, flops):
    out = jax.ShapeDtypeStruct((2, size, size), F32)
    return pl.pallas_call(
        kernel,
        out_shape=(out, out),
        in_specs=[VMEM] * len(operands),
        out_specs=(VMEM, VMEM),
        compiler_params=params(32),
        cost_estimate=cost(flops, 6_000_000),
        name=name,
    )(*operands)


def per_device(green_less, green_greater, offsets, orbitals, coulomb_diag, coulomb_up):
    size = coulomb_diag.shape[-1]
    cell, cells = lax.axis_index("cell"), lax.axis_size("cell")
    exchange = lambda x: lax.all_to_all(x, "energy", split_axis=0, concat_axis=0, tiled=True)

    chunk_a = exchange(polarize(True, offsets, green_less, green_greater))
    chunk_b = exchange(polarize(False, offsets, green_less, green_greater))
    prev_up = shift_cells(coulomb_up, 1)
    next_diag = shift_cells(coulomb_diag, -1)

    near = orbitals[jnp.clip(cell + jnp.arange(-1, 2, dtype=jnp.int32), 0, cells - 1)]
    last = jnp.where(cell < cells - 1, near[2], 0)
    sizes = jnp.concatenate([near, last[None]])
    diag, up, prev_u, prev_ut, next_d = prepare(sizes, coulomb_diag, coulomb_up, prev_up, next_diag)

    prev_a, next_a = shift_cells(chunk_a, 1), shift_cells(chunk_a, -1)
    prev_b, next_b = shift_cells(chunk_b, 1), shift_cells(chunk_b, -1)
    flops = 2 * 2 * size**3
    d, u = products(here_kernel, "here", (chunk_a, chunk_b, diag, up), size, 9 * flops)
    d, u = products(around_kernel, "around_a", (prev_a, next_a, up, prev_u, prev_ut, next_d, d, u), size, 9 * flops)
    d, u = products(around_kernel, "around_b", (prev_b, next_b, up, prev_u, prev_ut, next_d, d, u), size, 6 * flops)
    return d[:, None, None], u[:, None, None]


def solution(mesh):
    in_specs = (
        P(None, None, "cell", "energy", None),
        P(None, None, "cell", "energy", None),
        P(),
        P(),
        P("cell", None, None),
        P("cell", None, None),
    )
    out_specs = (P(None, "energy", "cell", None, None), P(None, "energy", "cell", None, None))
    return jax.shard_map(
        per_device, mesh=mesh, in_specs=in_specs, out_specs=out_specs, check_vma=False
    )
```

time: 127 us -> 80.1 us (0.63)
  local copies, waits for them, and re-layouts: 30.8 us -> 4.31 us
  matrix products: 22.7 us -> 0 us
  starting transfers between devices: 23.9 us -> 43 us
  other arithmetic: 18.2 us -> 0.09 us
  Pallas kernels: 0 us -> 15.3 us
  waiting for transfers between devices: 27.4 us -> 15.3 us
    dot_general x8 -> x0, matrix products: 22.7 us -> none  [the longest x3 10.8 us: right_mul_t(): return jnp.einsum('eij,kj->eik', blocks, coupling, precision=HIGH)]
    pallas_call x0 -> x6, Pallas kernels: none -> 15.3 us  [the longest x3 10.9 us: products(): pl.pallas_call(kernel, out_shape=(out, out), in_specs=[VMEM] * len(operan...]
    ppermute x2 -> x6, starting transfers between devices: 16.7 us -> 31.7 us  [shift_cells(): return lax.ppermute(block, 'cell', route)]
    gather x8 -> x1, local copies, waits for them, and re-layouts: 14.5 us -> 0.64 us  [per_device(): orbitals[jnp.clip(cell + jnp.arange(-1, 2, dtype=jnp.int32), 0, cells - 1)]]
    dynamic_slice x8 -> x0, local copies, waits for them, and re-layouts: 9.94 us -> none  [polarize(): return lax.map(single, offsets) / math.sqrt(count)]
    all_to_all x1 -> x2, waiting for transfers between devices: 23.8 us -> 15.3 us  [per_device(): lax.all_to_all(x, 'energy', split_axis=0, concat_axis=0, tiled=True)]
    select_n x16 -> x1, other arithmetic: 6.28 us -> 0.01 us  [per_device(): orbitals[jnp.clip(cell + jnp.arange(-1, 2, dtype=jnp.int32), 0, cells - 1)]]
    convert_element_type x9 -> x0, other arithmetic: 5.93 us -> none  [the longest x8 5.92 us: single(): weight = (source >= 0).astype(jnp.float32)]
  transfers between devices with their start and end apart: 3 -> 8, of which waited for: 2 -> 1; matrix products, arithmetic and copies ran while one was open for 18% -> 2% of each run, Pallas kernels for 0% -> 12%
where the time goes in v1:
time: 80.1 us; the launch traced here: 79.5 us
  starting transfers between devices  43 us (54%)
  Pallas kernels  15.3 us (19%)
  waiting for transfers between devices  15.3 us (19%)
  local copies, waits for them, and re-layouts  4.31 us (5%)
  between operations  1.5 us (2%)
    ppermute x6, starting transfers between devices, shift_cells(): return lax.ppermute(block, 'cell', route)  31.7 us
    all_to_all x2, waiting for transfers between devices, per_device(): lax.all_to_all(x, 'energy', split_axis=0, concat_axis=0, tiled=True)  15.3 us
    all_to_all x2, starting transfers between devices, per_device(): lax.all_to_all(x, 'energy', split_axis=0, concat_axis=0, tiled=True)  11.3 us
    pallas_call x3, Pallas kernels, products(): pl.pallas_call(kernel, out_shape=(out, out), in_specs=[VMEM] * len(operan...  10.9 us
    pallas_call x2, Pallas kernels, polarize(): pl.pallas_call(functools.partial(polar_kernel, first, count, rows), out_s...  3.34 us
    unnamed x18, local copies, waits for them, and re-layouts  3.09 us
  transfers between devices with their start and end apart: 8, of which 1 were waited for; matrix products, arithmetic and copies ran while one was open for 2% of the time, Pallas kernels for 12%

profile of v1, /device:TPU:6, one launch (start us, length us, event | category | flops | bytes accessed | tf_op | source)
XLA Modules:
  0.0 79.5 jit_solution(12727446094710104064)
XLA Ops:
  0.6 0.0 copy-start
  0.6 0.0 copy-start.1
  0.7 1.2 %copy-done.1 = f32[2,8,1,40,320]{4,3,2,1,0:T(8,128)S(1)} copy-done((f32[2,8,1,40,320]{4,3,2,1,0:T(8,128)S(1)}, f32[2,8,1,40,320]{4,3,2,1,0:T(8,128)}, u32[]{:S(2)}) %copy-start.1) | copy-done | bytes 819224
  1.9 1.2 %copy-done.3 = f32[2,8,1,40,320]{4,3,2,1,0:T(8,128)S(1)} copy-done((f32[2,8,1,40,320]{4,3,2,1,0:T(8,128)S(1)}, f32[2,8,1,40,320]{4,3,2,1,0:T(8,128)}, u32[]{:S(2)}) %copy-start.3) | copy-done | bytes 819224
  3.1 0.7 copy-done.7
  3.7 1.8 %polar_a.1 = f32[8,3,40,128]{3,2,1,0:T(8,128)} custom-call(s32[8]{0:T(128)S(1)} %copy-done.7, f32[2,8,1,40,320]{4,3,2,1,0:T(8,128)S(1)} %copy-done.1, f32[2,8,1,40,320]{4,3,2,1,0:T(8,128)S(1)} %copy-done.3), custom_call_target="tpu_custom_call" | custom-call | flops 4423680 | bytes 3000000 | tf_op jit(solution)/shard_map/polar_a/pallas_call | solution.py:74
  5.6 7.2 %all-to-all-start.1 = ((f32[8,3,40,128]{3,2,1,0:T(8,128)}), f32[8,3,40,128]{3,2,1,0:T(8,128)S(1)}, u32[]{:S(2)}, u32[]{:S(2)}) async-start(f32[8,3,40,128]{3,2,1,0:T(8,128)} %polar_a.1), calls=%async_computation.1 | async-start | bytes 983040 | tf_op jit(solution)/shard_map/all_to_all | solution.py:204
  12.8 0.0 copy-start.6
  12.8 1.5 %polar_b.1 = f32[8,2,40,128]{3,2,1,0:T(8,128)} custom-call(s32[8]{0:T(128)S(1)} %copy-done.8, f32[2,8,1,40,320]{4,3,2,1,0:T(8,128)S(1)} %copy-done.2, f32[2,8,1,40,320]{4,3,2,1,0:T(8,128)S(1)} %copy-done.4), custom_call_target="tpu_custom_call" | custom-call | flops 2949120 | bytes 3000000 | tf_op jit(solution)/shard_map/polar_b/pallas_call | solution.py:74
  14.3 15.3 %all-to-all-done.1.chunk_a = f32[8,3,40,128]{3,2,1,0:T(8,128)S(1)} async-done(((f32[8,3,40,128]{3,2,1,0:T(8,128)}), f32[8,3,40,128]{3,2,1,0:T(8,128)S(1)}, u32[]{:S(2)}, u32[]{:S(2)}) %all-to-all-start.1) | async-done | bytes 491552 | tf_op jit(solution)/shard_map/all_to_all | solution.py:204
  29.6 4.1 %all-to-all-start = ((f32[8,2,40,128]{3,2,1,0:T(8,128)}), f32[8,2,40,128]{3,2,1,0:T(8,128)}, u32[]{:S(2)}, u32[]{:S(2)}) async-start(f32[8,2,40,128]{3,2,1,0:T(8,128)} %polar_b.1), calls=%async_computation | async-start | bytes 655360 | tf_op jit(solution)/shard_map/all_to_all | solution.py:204
  33.7 1.9 %collective-permute-start.2 = (f32[1,320,320]{2,1,0:T(8,128)S(1)}, f32[1,320,320]{2,1,0:T(8,128)S(1)}, u32[]{:S(2)}, u32[]{:S(2)}) collective-permute-start(f32[1,320,320]{2,1,0:T(8,128)S(1)} %copy-done.6), channel_id=1, source_target_pairs={{0,1},{1,2},{2,3},{3,4},{4,5},{5,6},{6,7},{7,8},{8,9},{9,10},{10,1... | collective-permute-start | bytes 1228808 | tf_op jit(solution)/shard_map/ppermute | solution.py:28
  35.6 0.0 copy-done.5
  35.6 14.5 %collective-permute-start.3 = (f32[1,320,320]{2,1,0:T(8,128)S(1)}, f32[1,320,320]{2,1,0:T(8,128)S(1)}, u32[]{:S(2)}, u32[]{:S(2)}) collective-permute-start(f32[1,320,320]{2,1,0:T(8,128)S(1)} %copy-done.5), channel_id=1, source_target_pairs={{1,0},{2,1},{3,2},{4,3},{5,4},{6,5},{7,6},{8,7},{9,8},{10,9},{11,1... | collective-permute-start | bytes 1228808 | tf_op jit(solution)/shard_map/ppermute | solution.py:28
  50.1 1.9 %collective-permute-start.4 = (f32[8,3,40,128]{3,2,1,0:T(8,128)S(1)}, f32[8,3,40,128]{3,2,1,0:T(8,128)S(1)}, u32[]{:S(2)}, u32[]{:S(2)}) collective-permute-start(f32[8,3,40,128]{3,2,1,0:T(8,128)S(1)} %all-to-all-done.1.chunk_a), channel_id=1, source_target_pairs={{0,1},{1,2},{2,3},{3,4},{4,5},{5,6},{6,7},{7,8},{8,9},{9,10},{10,1... | collective-permute-start | bytes 1474568 | tf_op jit(solution)/shard_map/ppermute | solution.py:28
  52.0 5.8 %collective-permute-start.5 = (f32[8,3,40,128]{3,2,1,0:T(8,128)S(1)}, f32[8,3,40,128]{3,2,1,0:T(8,128)S(1)}, u32[]{:S(2)}, u32[]{:S(2)}) collective-permute-start(f32[8,3,40,128]{3,2,1,0:T(8,128)S(1)} %all-to-all-done.1.chunk_a), channel_id=1, source_target_pairs={{1,0},{2,1},{3,2},{4,3},{5,4},{6,5},{7,6},{8,7},{9,8},{10,9},{11,1... | collective-permute-start | bytes 1474568 | tf_op jit(solution)/shard_map/ppermute | solution.py:28
  57.8 0.6 gather_fusion
  58.5 0.6 slice.3
  59.7 0.0 all-to-all-done.chunk_b
  59.7 1.9 %collective-permute-start = (f32[8,2,40,128]{3,2,1,0:T(8,128)}, f32[8,2,40,128]{3,2,1,0:T(8,128)S(1)}, u32[]{:S(2)}, u32[]{:S(2)}) collective-permute-start(f32[8,2,40,128]{3,2,1,0:T(8,128)} %all-to-all-done.chunk_b), channel_id=1, source_target_pairs={{0,1},{1,2},{2,3},{3,4},{4,5},{5,6},{6,7},{7,8},{8,9},{9,10},{10,1... | collective-permute-start | bytes 983048 | tf_op jit(solution)/shard_map/ppermute | solution.py:28
  61.6 0.0 collective-permute-done.2.prev_up
  61.7 5.8 %collective-permute-start.1 = (f32[8,2,40,128]{3,2,1,0:T(8,128)}, f32[8,2,40,128]{3,2,1,0:T(8,128)S(1)}, u32[]{:S(2)}, u32[]{:S(2)}) collective-permute-start(f32[8,2,40,128]{3,2,1,0:T(8,128)} %all-to-all-done.chunk_b), channel_id=1, source_target_pairs={{1,0},{2,1},{3,2},{4,3},{5,4},{6,5},{7,6},{8,7},{9,8},{10,9},{11,1... | collective-permute-start | bytes 983048 | tf_op jit(solution)/shard_map/ppermute | solution.py:28
  67.4 0.1 pad_add_fusion.sizes
  67.5 0.0 collective-permute-done.3.next_diag
  67.5 1.1 %prep.1 = (bf16[2,320,320]{2,1,0:T(8,128)(2,1)S(1)}, bf16[2,320,320]{2,1,0:T(8,128)(2,1)S(1)}, bf16[2,320,320]{2,1,0:T(8,128)(2,1)S(1)}, bf16[2,320,320]{2,1,0:T(8,128)(2,1)S(1)}, bf16[2,320,320]{2,1,0:T(8,128)(2,1)S(1)}) custom-call(s32[4]{0:T(128)S(1)} %pad_add_fusion.sizes, f32[1,320,320]{2,1,0:T(8,128)S(1)} %copy-done.5, f32[1,320,320]{2,1,0:T(8,128)S(1)} %copy-done.6, ...), custom_call_target="tpu_custom_call" | custom-call | flops 4096000 | bytes 4096000 | tf_op jit(solution)/shard_map/prep/pallas_call | solution.py:121
  68.6 3.9 %here.1 = (f32[2,320,320]{2,1,0:T(8,128)S(1)}, f32[2,320,320]{2,1,0:T(8,128)S(1)}) custom-call(f32[8,3,40,128]{3,2,1,0:T(8,128)S(1)} %all-to-all-done.1.chunk_a, f32[8,2,40,128]{3,2,1,0:T(8,128)} %all-to-all-done.chunk_b, bf16[2,320,320]{2,1,0:T(8,128)(2,1)S(1)} %get-tuple-element.17.diag, bf16[2,320,320]{2,1,0:T(8,128)(2,1)S(1)} %get-tuple-element.13.up), custom_call_target="tpu_custom_call" | custom-call | flops 1179648000 | bytes 6000000 | tf_op jit(solution)/shard_map/here/pallas_call | solution.py:190
  72.4 0.0 collective-permute-done.4.prev_p
  72.4 0.0 collective-permute-done.5.next_p
  72.4 3.0 %around_a.1 = (f32[2,320,320]{2,1,0:T(8,128)S(1)}, f32[2,320,320]{2,1,0:T(8,128)S(1)}) custom-call(f32[8,3,40,128]{3,2,1,0:T(8,128)S(1)} %collective-permute-done.4.prev_p, f32[8,3,40,128]{3,2,1,0:T(8,128)S(1)} %collective-permute-done.5.next_p, bf16[2,320,320]{2,1,0:T(8,128)(2,1)S(1)} %get-tuple-element.13.up, ...), custom_call_target="tpu_custom_call" | custom-call | flops 1179648000 | bytes 6000000 | tf_op jit(solution)/shard_map/around_a/pallas_call | solution.py:190
  75.5 0.0 collective-permute-done.prev_p
  75.5 0.0 collective-permute-done.1.next_p
  75.5 4.1 %around_b.1 = (f32[2,320,320]{2,1,0:T(8,128)}, f32[2,320,320]{2,1,0:T(8,128)}) custom-call(f32[8,2,40,128]{3,2,1,0:T(8,128)S(1)} %collective-permute-done.prev_p, f32[8,2,40,128]{3,2,1,0:T(8,128)S(1)} %collective-permute-done.1.next_p, bf16[2,320,320]{2,1,0:T(8,128)(2,1)S(1)} %get-tuple-element.13.up, bf16[2,320,320]{2,1,0:T(8,128)(2,1)S(1)} %get-tuple-element.14.prev_up, ...), custom_call_target="tpu_custom_call" | custom-call | flops 786432000 | bytes 6000000 | tf_op jit(solution)/shard_map/around_b/pallas_call | solution.py:190
  (13 shorter events, 0.0 us)
Async XLA Ops:
  0.6 57.2 %copy-start = (s32[96]{0:T(128)S(1)}, s32[96]{0:T(128)}, u32[]{:S(2)}) copy-start(s32[96]{0:T(128)} %param.9) | copy-start | bytes 1156
  0.6 1.2 %copy-start.1 = (f32[2,8,1,40,320]{4,3,2,1,0:T(8,128)S(1)}, f32[2,8,1,40,320]{4,3,2,1,0:T(8,128)}, u32[]{:S(2)}) copy-start(f32[2,8,1,40,320]{4,3,2,1,0:T(8,128)} %less.3) | copy-start | bytes 2457604
  1.9 1.2 %copy-start.3 = (f32[2,8,1,40,320]{4,3,2,1,0:T(8,128)S(1)}, f32[2,8,1,40,320]{4,3,2,1,0:T(8,128)}, u32[]{:S(2)}) copy-start(f32[2,8,1,40,320]{4,3,2,1,0:T(8,128)} %greater.3) | copy-start | bytes 2457604
  3.1 0.7 copy-start.7
  3.7 9.1 %copy-start.4 = (f32[2,8,1,40,320]{4,3,2,1,0:T(8,128)S(1)}, f32[2,8,1,40,320]{4,3,2,1,0:T(8,128)}, u32[]{:S(2)}) copy-start(f32[2,8,1,40,320]{4,3,2,1,0:T(8,128)} %greater.3) | copy-start | bytes 2457604
  3.7 9.1 %copy-start.8 = (s32[8]{0:T(128)S(1)}, s32[8]{0:T(128)}, u32[]{:S(2)}) copy-start(s32[8]{0:T(128)} %offsets.3) | copy-start | bytes 100
  5.6 7.3 %copy-start.2 = (f32[2,8,1,40,320]{4,3,2,1,0:T(8,128)S(1)}, f32[2,8,1,40,320]{4,3,2,1,0:T(8,128)}, u32[]{:S(2)}) copy-start(f32[2,8,1,40,320]{4,3,2,1,0:T(8,128)} %less.3) | copy-start | bytes 2457604
  5.6 24.0 %all-to-all-start.1 = ((f32[8,3,40,128]{3,2,1,0:T(8,128)}), f32[8,3,40,128]{3,2,1,0:T(8,128)S(1)}, u32[]{:S(2)}, u32[]{:S(2)}) async-start(f32[8,3,40,128]{3,2,1,0:T(8,128)} %polar_a.1), calls=%async_computation.1 | async-start | bytes 983040 | tf_op jit(solution)/shard_map/all_to_all | solution.py:204
  12.8 20.8 %copy-start.6 = (f32[1,320,320]{2,1,0:T(8,128)S(1)}, f32[1,320,320]{2,1,0:T(8,128)}, u32[]{:S(2)}) copy-start(f32[1,320,320]{2,1,0:T(8,128)} %up.1) | copy-start | bytes 1228804
  14.3 21.3 %copy-start.5 = (f32[1,320,320]{2,1,0:T(8,128)S(1)}, f32[1,320,320]{2,1,0:T(8,128)}, u32[]{:S(2)}) copy-start(f32[1,320,320]{2,1,0:T(8,128)} %diag.1) | copy-start | bytes 1228804
  29.6 30.1 %all-to-all-start = ((f32[8,2,40,128]{3,2,1,0:T(8,128)}), f32[8,2,40,128]{3,2,1,0:T(8,128)}, u32[]{:S(2)}, u32[]{:S(2)}) async-start(f32[8,2,40,128]{3,2,1,0:T(8,128)} %polar_b.1), calls=%async_computation | async-start | bytes 655360 | tf_op jit(solution)/shard_map/all_to_all | solution.py:204
  33.7 28.0 %collective-permute-start.2 = (f32[1,320,320]{2,1,0:T(8,128)S(1)}, f32[1,320,320]{2,1,0:T(8,128)S(1)}, u32[]{:S(2)}, u32[]{:S(2)}) collective-permute-start(f32[1,320,320]{2,1,0:T(8,128)S(1)} %copy-done.6), channel_id=1, source_target_pairs={{0,1},{1,2},{2,3},{3,4},{4,5},{5,6},{6,7},{7,8},{8,9},{9,10},{10,1... | collective-permute-start | bytes 1228808 | tf_op jit(solution)/shard_map/ppermute | solution.py:28
  35.6 31.9 %collective-permute-start.3 = (f32[1,320,320]{2,1,0:T(8,128)S(1)}, f32[1,320,320]{2,1,0:T(8,128)S(1)}, u32[]{:S(2)}, u32[]{:S(2)}) collective-permute-start(f32[1,320,320]{2,1,0:T(8,128)S(1)} %copy-done.5), channel_id=1, source_target_pairs={{1,0},{2,1},{3,2},{4,3},{5,4},{6,5},{7,6},{8,7},{9,8},{10,9},{11,1... | collective-permute-start | bytes 1228808 | tf_op jit(solution)/shard_map/ppermute | solution.py:28
  50.1 22.3 %collective-permute-start.4 = (f32[8,3,40,128]{3,2,1,0:T(8,128)S(1)}, f32[8,3,40,128]{3,2,1,0:T(8,128)S(1)}, u32[]{:S(2)}, u32[]{:S(2)}) collective-permute-start(f32[8,3,40,128]{3,2,1,0:T(8,128)S(1)} %all-to-all-done.1.chunk_a), channel_id=1, source_target_pairs={{0,1},{1,2},{2,3},{3,4},{4,5},{5,6},{6,7},{7,8},{8,9},{9,10},{10,1... | collective-permute-start | bytes 1474568 | tf_op jit(solution)/shard_map/ppermute | solution.py:28
  52.0 20.4 %collective-permute-start.5 = (f32[8,3,40,128]{3,2,1,0:T(8,128)S(1)}, f32[8,3,40,128]{3,2,1,0:T(8,128)S(1)}, u32[]{:S(2)}, u32[]{:S(2)}) collective-permute-start(f32[8,3,40,128]{3,2,1,0:T(8,128)S(1)} %all-to-all-done.1.chunk_a), channel_id=1, source_target_pairs={{1,0},{2,1},{3,2},{4,3},{5,4},{6,5},{7,6},{8,7},{9,8},{10,9},{11,1... | collective-permute-start | bytes 1474568 | tf_op jit(solution)/shard_map/ppermute | solution.py:28
  59.7 15.7 %collective-permute-start = (f32[8,2,40,128]{3,2,1,0:T(8,128)}, f32[8,2,40,128]{3,2,1,0:T(8,128)S(1)}, u32[]{:S(2)}, u32[]{:S(2)}) collective-permute-start(f32[8,2,40,128]{3,2,1,0:T(8,128)} %all-to-all-done.chunk_b), channel_id=1, source_target_pairs={{0,1},{1,2},{2,3},{3,4},{4,5},{5,6},{6,7},{7,8},{8,9},{9,10},{10,1... | collective-permute-start | bytes 983048 | tf_op jit(solution)/shard_map/ppermute | solution.py:28
  61.7 13.8 %collective-permute-start.1 = (f32[8,2,40,128]{3,2,1,0:T(8,128)}, f32[8,2,40,128]{3,2,1,0:T(8,128)S(1)}, u32[]{:S(2)}, u32[]{:S(2)}) collective-permute-start(f32[8,2,40,128]{3,2,1,0:T(8,128)} %all-to-all-done.chunk_b), channel_id=1, source_target_pairs={{1,0},{2,1},{3,2},{4,3},{5,4},{6,5},{7,6},{8,7},{9,8},{10,9},{11,1... | collective-permute-start | bytes 983048 | tf_op jit(solution)/shard_map/ppermute | solution.py:28
